TPU v7x, 256 devices: a whole 4x4x8 slice. The times are simulated.
256 devices in a mesh: frames: 32 (over y, z_lo, x), space: 8 (over z_hi, core).
Axes of the slice: x: 4, y: 4, z: 8 (z_hi: 4, z_lo: 2; z = z_hi * 2 + z_lo), core: 2. Of those that a mesh axis runs over, the one named last changes fastest.
Arguments:
- latents: bfloat16 [32, 3584, 1152], P('frames', 'space'), may hold values from -6 to 6
- merge_slot: int32 [32, 3584], P('frames', 'space'), may hold values from 0 to 1791, as said below
- modulation: float32 [6, 1152], replicated, may hold values from -3 to 3
- spatial_qkv: bfloat16 [1152, 1728], replicated, may hold values from -0.41247896 to 0.41247896
- spatial_proj: bfloat16 [576, 1152], replicated, may hold values from -0.25 to 0.25
- temporal_qkv: bfloat16 [1152, 1728], replicated, may hold values from -0.41247896 to 0.41247896
- temporal_proj: bfloat16 [576, 1152], replicated, may hold values from -0.25 to 0.25
Outputs:
- block_out: bfloat16 [32, 3584, 1152], P('frames', 'space')
Inputs may be any that keep to these rules, and one draw needn't show every extreme that they name: `merge_slot`: within each frame, the tokens of the k-th aligned block of 448 tokens join merged tokens k * 224 to (k + 1) * 224 - 1 only, and every merged token is joined by at least one token.
All inputs are finite; a program needn't handle non-finite values.
Results may differ from a plain program's by a relative error of at most 0.0062.
Values may be sent and summed in bfloat16 or wider, within the bound.
A program may use at most 128 MiB of HBM per device.

v0:
```python
import math
import jax
import jax.numpy as jnp
from jax import lax
from jax.sharding import PartitionSpec as P

HEADS = 8
HD = 72


def layer_norm(values):
    values = values.astype(jnp.float32)
    center = values - jnp.mean(values, -1, keepdims=True)
    spread = jnp.mean(center * center, -1, keepdims=True)
    return center * lax.rsqrt(spread + 1e-06)


def modulate(values, modulation, which):
    return (layer_norm(values) * (1.0 + modulation[which + 1]) + modulation[which]).astype(
        jnp.bfloat16
    )


def shards(latents, merge_slot, modulation, spatial_qkv, spatial_proj, temporal_qkv, temporal_proj):
    row_count = latents.shape[1]
    slot_count = row_count // 2
    width = latents.shape[2]
    inner = spatial_proj.shape[0]
    root_size = math.sqrt(HD)
    own_rows = latents[0]
    normed = modulate(own_rows, modulation, 0)
    local_slot = merge_slot[0] - lax.axis_index("space") * slot_count
    one_hot = (local_slot[:, None] == jnp.arange(slot_count, dtype=jnp.int32)[None, :]).astype(
        jnp.bfloat16
    )
    counts = jnp.sum(one_hot.astype(jnp.float32), 0)
    summed = lax.dot_general(
        one_hot, normed, (((0,), (0,)), ((), ())), preferred_element_type=jnp.float32
    )
    merged = (summed / counts[:, None]).astype(jnp.bfloat16)
    projected = jnp.dot(merged, spatial_qkv, preferred_element_type=jnp.float32).astype(
        jnp.bfloat16
    )
    query_rows = projected[:, :inner]
    key_rows = projected[:, inner : 2 * inner]
    value_rows = projected[:, 2 * inner :]
    query_heads = query_rows.reshape(slot_count, HEADS, HD)
    pieces = (
        lax.all_gather(key_rows, "space", axis=0, tiled=True),
        lax.all_gather(value_rows, "space", axis=0, tiled=True),
    )
    run_peak = jnp.full((HEADS, slot_count), -1e30, jnp.float32)
    key_part = pieces[0].reshape(pieces[0].shape[0], HEADS, HD)
    value_part = pieces[1].reshape(pieces[1].shape[0], HEADS, HD)
    scores = (
        jnp.einsum("qhd,khd->hqk", query_heads, key_part, preferred_element_type=jnp.float32)
        / root_size
    )
    new_peak = jnp.maximum(run_peak, jnp.max(scores, -1))
    weights = jnp.exp(scores - new_peak[..., None])
    run_total = jnp.sum(weights, -1)
    run_sum = jnp.einsum(
        "hqk,khd->hqd", weights.astype(jnp.bfloat16), value_part, preferred_element_type=jnp.float32
    )
    run_peak, run_total, run_sum = (new_peak, run_total, run_sum)
    attended = (
        (run_sum / run_total[..., None])
        .transpose(1, 0, 2)
        .reshape(slot_count, inner)
        .astype(jnp.bfloat16)
    )
    spatial_out = jnp.dot(attended, spatial_proj, preferred_element_type=jnp.float32).astype(
        jnp.bfloat16
    )
    spread_back = jnp.dot(one_hot, spatial_out, preferred_element_type=jnp.float32)
    after_spatial = (own_rows.astype(jnp.float32) + modulation[2] * spread_back).astype(
        jnp.bfloat16
    )
    by_place = lax.all_to_all(
        after_spatial[None], "frames", split_axis=1, concat_axis=0, tiled=True
    )
    frame_count = by_place.shape[0]
    place_count = by_place.shape[1]
    flat = by_place.reshape(frame_count * place_count, width)
    normed_time = modulate(flat, modulation, 3)
    projected_time = jnp.dot(normed_time, temporal_qkv, preferred_element_type=jnp.float32).astype(
        jnp.bfloat16
    )
    split = projected_time.reshape(frame_count, place_count, 3, HEADS, HD)
    scores_time = (
        jnp.einsum(
            "flhd,glhd->lhfg", split[:, :, 0], split[:, :, 1], preferred_element_type=jnp.float32
        )
        / root_size
    )
    weights_time = jnp.exp(scores_time - jnp.max(scores_time, -1, keepdims=True))
    total_time = jnp.sum(weights_time, -1)
    mixture_time = (
        jnp.einsum(
            "lhfg,glhd->flhd",
            weights_time.astype(jnp.bfloat16),
            split[:, :, 2],
            preferred_element_type=jnp.float32,
        )
        / total_time.transpose(2, 0, 1)[..., None]
    )
    attended_time = mixture_time.astype(jnp.bfloat16).reshape(frame_count * place_count, inner)
    branch = jnp.dot(attended_time, temporal_proj, preferred_element_type=jnp.float32)
    finished = (
        (flat.astype(jnp.float32) + modulation[5] * branch)
        .astype(jnp.bfloat16)
        .reshape(frame_count, place_count, width)
    )
    return lax.all_to_all(finished, "frames", split_axis=0, concat_axis=1, tiled=True)


def solution(mesh):
    placed = (P("frames", "space", None), P("frames", "space"), P(), P(), P(), P(), P())
    return jax.shard_map(
        shards, mesh=mesh, in_specs=placed, out_specs=P("frames", "space", None), check_vma=False
    )
```

profile of v0, /device:TPU:2, one launch (start us, length us, event | category | flops | bytes accessed | tf_op | source)
XLA Modules:
  0.0 201.5 jit_solution(2372403140848422935)
XLA Ops:
  6.5 1.8 slice_reduce_fusion.1
  8.3 0.7 broadcast_subtract_fusion
  9.2 1.4 convert_reduce_fusion.1
  10.6 1.6 fusion.16
  12.3 4.1 %convolution_convert_fusion.2 = bf16[224,1728]{1,0:T(8,128)(2,1)S(1)} fusion(bf16[1152,1728]{0,1:T(8,128)(2,1)} %param.10, bf16[1,448,1152]{2,1,0:T(8,128)(2,1)S(1)} %copy-done.2, f32[1152]{0:T(1024)S(1)} %get-tuple-element.6, f32[1152]{0:T(1024)S(1)} %get-tuple-element.7, f32[448]{0:T(512)S(1)} %add_rsqrt_fusion.1, f32[448]{0:T(512)S(1)} %broadcast_multiply_fusion.1, ...), kind=kOutput, calls=%fused_computation.24 | convolution fusion | flops 1127124992 | bytes 5803136 | tf_op jit(solution)/shard_map/dot_general | solution.py:41
  16.4 0.9 fusion.62
  17.4 0.7 all-gather.5.cloned.1.call-update
  18.1 0.9 copy.33
  18.9 39.3 %all-gather.3.cloned.1.call-done = bf16[1792,576]{1,0:T(8,128)(2,1)} async-done(((bf16[224,576]{1,0:T(8,128)(2,1)}), bf16[1792,576]{1,0:T(8,128)(2,1)}) %all-gather.3.cloned.1.call-update) | async-done | bytes 2064400 | tf_op jit(solution)/shard_map/all_gather | solution.py:49
  58.2 3.0 %copy.34 = bf16[1792,576]{0,1:T(8,128)(2,1)S(1)} copy(bf16[1792,576]{1,0:T(8,128)(2,1)} %all-gather.3.cloned.1.call-done) | data formatting | bytes 4128768 | tf_op jit(solution)/shard_map/all_gather | solution.py:49
  61.2 2.9 %multiply_reduce_fusion = (f32[8,224]{1,0:T(8,128)S(1)}, f32[8,224,1792]{2,1,0:T(8,128)S(1)}) fusion(bf16[224,8,72]{0,2,1:T(8,128)(2,1)} %bitcast.87, bf16[1792,8,72]{0,2,1:T(8,128)(2,1)S(1)} %bitcast.83), kind=kOutput, calls=%fused_computation.1 | convolution fusion | flops 468842752 | bytes 15174656 | tf_op jit(solution)/shard_map/qhd,khd->hqk/dot_general | solution.py:56
  64.2 4.6 %copy-done.1 = f32[8,224,1792]{2,1,0:T(8,128)} copy-done((f32[8,224,1792]{2,1,0:T(8,128)}, f32[8,224,1792]{2,1,0:T(8,128)S(1)}, u32[]{:S(2)}) %copy-start.1) | copy-done | bytes 12845080
  68.8 2.3 %fusion = f32[8,224]{1,0:T(8,128)S(1)} fusion(f32[8,224,1792]{2,1,0:T(8,128)S(1)} %get-tuple-element.20, f32[8,224]{1,0:T(8,128)S(1)} %broadcast_maximum_fusion), kind=kLoop, calls=%fused_computation.2 | loop fusion | flops 9632000 | bytes 12859392 | tf_op jit(solution)/shard_map/reduce_sum | solution.py:61
  71.1 24.5 %all-gather.5.cloned.1.call-done = bf16[1792,576]{1,0:T(8,128)(2,1)} async-done(((bf16[224,576]{1,0:T(8,128)(2,1)}), bf16[1792,576]{1,0:T(8,128)(2,1)}) %all-gather.5.cloned.1.call-update) | async-done | bytes 2064400 | tf_op jit(solution)/shard_map/all_gather | solution.py:50
  95.6 4.1 %copy.35 = bf16[1792,576]{0,1:T(8,128)(2,1)} copy(bf16[1792,576]{1,0:T(8,128)(2,1)} %all-gather.5.cloned.1.call-done) | data formatting | bytes 4128768 | tf_op jit(solution)/shard_map/all_gather | solution.py:50
  99.7 7.8 %fusion.45 = bf16[224,8,72]{0,2,1:T(8,128)(2,1)S(1)} fusion(bf16[1792,8,72]{0,2,1:T(8,128)(2,1)} %bitcast.86, f32[8,224,1792]{2,1,0:T(8,128)} %copy-done.1, f32[8,224]{1,0:T(8,128)S(1)} %broadcast_maximum_fusion, f32[224,8]{0,1:T(8,128)S(1)} %bitcast.89), kind=kOutput, calls=%fused_computation.54 | convolution fusion | flops 472313856 | bytes 15181824 | tf_op jit(solution)/shard_map/hqk,khd->hqd/dot_general | solution.py:62
  107.5 2.0 fusion.10
  109.5 2.8 %copy.59 = bf16[1,448,1152]{2,0,1:T(2,128)(2,1)S(1)} copy(bf16[1,448,1152]{2,1,0:T(8,128)(2,1)} %fusion.10) | data formatting | bytes 2064384 | tf_op jit(solution)/shard_map/broadcast_in_dim | solution.py:80
  112.9 7.9 %reduce.17 = bf16[448,1152]{1,0:T(8,128)(2,1)} reduce(bf16[448,1,1152]{2,1,0:T(2,128)(2,1)S(1)} %bitcast.84, bf16[]{:T(256)} %broadcast.86), dimensions={1}, to_apply=%bitcast.82.reduce_sub_computation | reduce | bytes 2064386
  120.8 2.5 %reshape.108 = bf16[32,2,8064]{2,1,0:T(2,128)(2,1)S(1)} reshape(bf16[448,1152]{1,0:T(8,128)(2,1)} %reduce.17) | data formatting | bytes 2064384
  123.3 23.9 %all_to_all.21 = bf16[32,2,8064]{2,1,0:T(2,128)(2,1)} all-to-all(bf16[32,2,8064]{2,1,0:T(2,128)(2,1)S(1)} %reshape.108), channel_id=1, replica_groups=mesh['frames'=32,'space'=8] {'frames'}, dimensions={0} | all-to-all | bytes 2064384 | tf_op jit(solution)/shard_map/all_to_all | solution.py:79
  147.2 4.2 %reshape.109 = bf16[448,1,1152]{2,1,0:T(2,128)(2,1)S(1)} reshape(bf16[32,2,8064]{2,1,0:T(2,128)(2,1)} %all_to_all.21) | data formatting | bytes 2064384
  152.6 1.3 copy-done.9
  153.9 2.4 %convolution_convert_fusion = bf16[448,1728]{1,0:T(8,128)(2,1)S(1)} fusion(bf16[1152,1728]{0,1:T(8,128)(2,1)S(1)} %copy-done.9, bf16[1,448,1152]{2,1,0:T(8,128)(2,1)S(1)} %get-tuple-element.12, f32[1152]{0:T(1024)S(1)} %copy-done.6, f32[1152]{0:T(1024)S(1)} %copy-done.7, f32[448]{0:T(512)S(1)} %add_rsqrt_fusion, f32[448]{0:T(512)S(1)} %broadcast_multiply_fusion), kind=kOutput, calls=%fused_computation.14 | convolution fusion | flops 1787498496 | bytes 6574592 | tf_op jit(solution)/shard_map/dot_general | solution.py:86
  156.3 4.0 %reshape.98 = bf16[32,14,3,8,72]{4,3,2,1,0:T(8,128)(2,1)} reshape(bf16[448,1728]{1,0:T(8,128)(2,1)S(1)} %convolution_convert_fusion) | data formatting | bytes 3096576 | tf_op jit(solution)/shard_map/reshape | solution.py:89
  160.3 1.9 fusion.61
  162.2 0.6 multiply_reduce_fusion.1
  163.5 1.1 fusion.26
  164.9 1.5 reshape.99
  166.5 2.5 %fusion.8 = bf16[448,1152]{1,0:T(8,128)(2,1)S(1)} fusion(bf16[448,576]{1,0:T(8,128)(2,1)} %reshape.99, bf16[576,1152]{1,0:T(8,128)(2,1)} %param.13, bf16[1,448,1152]{2,1,0:T(8,128)(2,1)S(1)} %copy-done.5, f32[1152]{0:T(1024)S(1)} %get-tuple-element.5), kind=kOutput, calls=%fused_computation.15 | convolution fusion | flops 596606976 | bytes 3912192 | tf_op jit(solution)/shard_map/dot_general | solution.py:108
  169.4 23.1 %all_to_all.22 = bf16[32,14,1152]{2,1,0:T(8,128)(2,1)} all-to-all(bf16[32,14,1152]{2,1,0:T(8,128)(2,1)S(1)} %reshape.100), channel_id=1, replica_groups=mesh['frames'=32,'space'=8] {'frames'}, dimensions={0} | all-to-all | bytes 2064384 | tf_op jit(solution)/shard_map/all_to_all | solution.py:114
  192.5 2.2 %all_to_all.8 = bf16[1,448,1152]{2,1,0:T(8,128)(2,1)} reshape(bf16[32,14,1152]{2,1,0:T(8,128)(2,1)} %all_to_all.22) | data formatting | bytes 2064384 | tf_op jit(solution)/shard_map/all_to_all | solution.py:114
  (33 shorter events, 3.3 us)
Async XLA Ops:
  6.5 100.9 %copy-start = (bf16[576,1152]{1,0:T(8,128)(2,1)S(1)}, bf16[576,1152]{1,0:T(8,128)(2,1)}, u32[]{:S(2)}) copy-start(bf16[576,1152]{1,0:T(8,128)(2,1)} %param.11) | copy-start | bytes 3981316
  6.5 5.7 %copy-start.2 = (bf16[1,448,1152]{2,1,0:T(8,128)(2,1)S(1)}, bf16[1,448,1152]{2,1,0:T(8,128)(2,1)}, u32[]{:S(2)}) copy-start(bf16[1,448,1152]{2,1,0:T(8,128)(2,1)} %param.7) | copy-start | bytes 3096580
  6.5 51.7 %all-gather.3.cloned.1.call-start = ((), (), s32[]{:S(2)}) async-start(), calls=%async_computation.2 | async-start | bytes 2580480 | tf_op jit(solution)/shard_map/all_gather | solution.py:49
  17.3 78.2 %all-gather.5.cloned.1.call-start = ((), (), s32[]{:S(2)}) async-start(), calls=%async_computation.3 | async-start | bytes 2580480 | tf_op jit(solution)/shard_map/all_gather | solution.py:50
  64.2 4.6 %copy-start.1 = (f32[8,224,1792]{2,1,0:T(8,128)}, f32[8,224,1792]{2,1,0:T(8,128)S(1)}, u32[]{:S(2)}) copy-start(f32[8,224,1792]{2,1,0:T(8,128)S(1)} %get-tuple-element.20) | copy-start | bytes 38535172
  99.7 7.8 %copy-start.3 = (bf16[1,448,1152]{2,1,0:T(8,128)(2,1)S(1)}, bf16[1,448,1152]{2,1,0:T(8,128)(2,1)}, u32[]{:S(2)}) copy-start(bf16[1,448,1152]{2,1,0:T(8,128)(2,1)} %param.7) | copy-start | bytes 3096580
  99.7 7.8 %copy-start.8 = (f32[1152]{0:T(1024)S(1)}, f32[1152]{0:T(1024)}, u32[]{:S(2)}) copy-start(f32[1152]{0:T(1024)} %get-tuple-element.8) | copy-start | bytes 13828
  151.4 1.2 copy-start.6
  151.4 1.2 copy-start.7
  151.4 2.5 %copy-start.9 = (bf16[1152,1728]{0,1:T(8,128)(2,1)S(1)}, bf16[1152,1728]{0,1:T(8,128)(2,1)}, u32[]{:S(2)}) copy-start(bf16[1152,1728]{0,1:T(8,128)(2,1)} %param.12) | copy-start | bytes 11943940
  151.6 1.0 copy-start.4
  164.6 1.9 copy-start.5
Sparse Core Ops, SparseCore 0:
  17.4 40.7 all-gather.2
  60.1 35.4 all-gather.4
where the time goes:
time: 202 us; the launch traced here: 201 us
  waiting for transfers between devices  64.5 us (32%)
  blocking collectives  47 us (23%)
  local copies, waits for them, and re-layouts  35.6 us (18%)
  matrix products  23.5 us (12%)
  other arithmetic  17.2 us (9%)
  between operations  13.6 us (7%)
    all_gather x1, waiting for transfers between devices, shards(): lax.all_gather(key_rows, 'space', axis=0, tiled=True)  39.3 us
    all_gather x1, waiting for transfers between devices, shards(): lax.all_gather(value_rows, 'space', axis=0, tiled=True)  24.5 us
    all_to_all x1, blocking collectives, shards(): lax.all_to_all(after_spatial[None], 'frames', split_axis=1, concat_axis=0...  23.9 us
    all_to_all x1, blocking collectives, shards(): lax.all_to_all(finished, 'frames', split_axis=0, concat_axis=1, tiled=True)  23.1 us
    unnamed x23, local copies, waits for them, and re-layouts  13.7 us
    unnamed x1, other arithmetic  7.93 us
    dot_general x1, matrix products, shards(): jnp.einsum('hqk,khd->hqd', weights.astype(jnp.bfloat16), value_part, pref...  7.79 us
    all_gather x1, local copies, waits for them, and re-layouts, shards(): lax.all_gather(value_rows, 'space', axis=0, tiled=True)  4.13 us
  transfers between devices with their start and end apart: 2, of which 2 were waited for; matrix products, arithmetic and copies ran while one was open for 5% of the time, Pallas kernels for 0%

commit v1 on v0

--- a/solution.py
+++ b/solution.py
@@ -47,7 +47,9 @@
     query_heads = query_rows.reshape(slot_count, HEADS, HD)
     pieces = (
         lax.all_gather(key_rows, "space", axis=0, tiled=True),
-        lax.all_gather(value_rows, "space", axis=0, tiled=True),
+        jnp.concatenate(
+            lax.all_to_all(jnp.stack([value_rows] * lax.axis_size("space")), "space", 0, 0), axis=0
+        ),
     )
     run_peak = jnp.full((HEADS, slot_count), -1e30, jnp.float32)
     key_part = pieces[0].reshape(pieces[0].shape[0], HEADS, HD)

time: 202 us -> 217 us (1.074); the launches traced: 201 us -> 214 us
  starting transfers between devices: 0.04 us -> 8.51 us
  blocking collectives: 47 us -> 40.4 us
  waiting for transfers between devices: 64.5 us -> 70.3 us
  local copies, waits for them, and re-layouts: 35.6 us -> 41.1 us
    all_to_all x0 -> x1, waiting for transfers between devices: none -> 69.6 us  [shards(): lax.all_to_all(jnp.stack([value_rows] * lax.axis_size('space')), 'space',...]
    all_gather x1, waiting for transfers between devices: 39.3 us -> 0.01 us  [shards(): lax.all_gather(key_rows, 'space', axis=0, tiled=True)]
    all_gather x1 -> x0, waiting for transfers between devices: 24.5 us -> none  [shards(): lax.all_gather(value_rows, 'space', axis=0, tiled=True)]
    all_to_all x0 -> x1, starting transfers between devices: none -> 8.47 us  [shards(): lax.all_to_all(jnp.stack([value_rows] * lax.axis_size('space')), 'space',...]
    another operation x0 -> x2, local copies, waits for them, and re-layouts: none -> 6.92 us  [the longest x1 5.35 us: shards(): value_part = pieces[1].reshape(pieces[1].shape[0], HEADS, HD)]
    all_to_all x0 -> x1, local copies, waits for them, and re-layouts: none -> 4.81 us  [shards(): lax.all_to_all(jnp.stack([value_rows] * lax.axis_size('space')), 'space',...]
    all_to_all x1, blocking collectives: 23.1 us -> 18.5 us  [shards(): lax.all_to_all(finished, 'frames', split_axis=0, concat_axis=1, tiled=True)]
    all_gather x1 -> x0, local copies, waits for them, and re-layouts: 4.13 us -> none  [shards(): lax.all_gather(value_rows, 'space', axis=0, tiled=True)]
  transfers between devices with their start and end apart: 2 -> 2, of which waited for: 2 -> 1; matrix products, arithmetic and copies ran while one was open for 5% -> 5% of each run, Pallas kernels for 0% -> 0%
where the time goes in v1:
time: 217 us; the launch traced here: 214 us
  waiting for transfers between devices  70.3 us (32%)
  local copies, waits for them, and re-layouts  41.1 us (19%)
  blocking collectives  40.4 us (19%)
  matrix products  23.5 us (11%)
  other arithmetic  16.6 us (8%)
  between operations  13.6 us (6%)
  starting transfers between devices  8.51 us (4%)
    all_to_all x1, waiting for transfers between devices, shards(): lax.all_to_all(jnp.stack([value_rows] * lax.axis_size('space')), 'space',...  69.6 us
    all_to_all x1, blocking collectives, shards(): lax.all_to_all(after_spatial[None], 'frames', split_axis=1, concat_axis=0...  22 us
    all_to_all x1, blocking collectives, shards(): lax.all_to_all(finished, 'frames', split_axis=0, concat_axis=1, tiled=True)  18.5 us
    unnamed x25, local copies, waits for them, and re-layouts  11.4 us
    all_to_all x1, starting transfers between devices, shards(): lax.all_to_all(jnp.stack([value_rows] * lax.axis_size('space')), 'space',...  8.47 us
    unnamed x1, other arithmetic  8.15 us
    dot_general x1, matrix products, shards(): jnp.einsum('hqk,khd->hqd', weights.astype(jnp.bfloat16), value_part, pref...  7.78 us
    another operation x1, local copies, waits for them, and re-layouts, shards(): value_part = pieces[1].reshape(pieces[1].shape[0], HEADS, HD)  5.35 us
  transfers between devices with their start and end apart: 2, of which 1 were waited for; matrix products, arithmetic and copies ran while one was open for 5% of the time, Pallas kernels for 0%

profile of v1, /device:TPU:2, one launch (start us, length us, event | category | flops | bytes accessed | tf_op | source)
XLA Modules:
  0.0 214.1 jit_solution(2839947630310181183)
XLA Ops:
  6.5 1.7 slice_reduce_fusion.1
  8.2 1.4 convert_reduce_fusion.1
  9.7 1.6 fusion.16
  11.5 4.1 %convolution_convert_fusion.2 = bf16[224,1728]{1,0:T(8,128)(2,1)S(1)} fusion(bf16[1152,1728]{0,1:T(8,128)(2,1)} %param.10, bf16[1,448,1152]{2,1,0:T(8,128)(2,1)S(1)} %copy-done.2, f32[1152]{0:T(1024)S(1)} %get-tuple-element.6, f32[1152]{0:T(1024)S(1)} %get-tuple-element.7, f32[448]{0:T(512)S(1)} %add_rsqrt_fusion.1, f32[448]{0:T(512)S(1)} %broadcast_multiply_fusion.1, ...), kind=kOutput, calls=%fused_computation.24 | convolution fusion | flops 1127124992 | bytes 5803136 | tf_op jit(solution)/shard_map/dot_general | solution.py:41
  15.6 0.9 fusion.62
  16.5 1.6 stack.2
  18.1 8.5 %all-to-all-start = ((bf16[8,224,576]{2,1,0:T(8,128)(2,1)}), bf16[8,224,576]{2,1,0:T(8,128)(2,1)}, u32[]{:S(2)}, u32[]{:S(2)}) async-start(bf16[8,224,576]{2,1,0:T(8,128)(2,1)} %stack.2), calls=%async_computation | async-start | bytes 4587520 | tf_op jit(solution)/shard_map/all_to_all | solution.py:51
  26.6 0.7 all-gather.2.cloned.1.call-update
  27.3 0.9 copy.33
  28.1 69.6 %all-to-all-done = bf16[8,224,576]{2,1,0:T(8,128)(2,1)} async-done(((bf16[8,224,576]{2,1,0:T(8,128)(2,1)}), bf16[8,224,576]{2,1,0:T(8,128)(2,1)}, u32[]{:S(2)}, u32[]{:S(2)}) %all-to-all-start) | async-done | bytes 2064416 | tf_op jit(solution)/shard_map/all_to_all | solution.py:51
  97.8 4.8 %copy.35 = bf16[8,224,576]{1,0,2:T(8,128)(2,1)} copy(bf16[8,224,576]{2,1,0:T(8,128)(2,1)} %all-to-all-done) | data formatting | bytes 4128768 | tf_op jit(solution)/shard_map/all_to_all | solution.py:51
  102.6 5.4 %reshape_reshape.3 = bf16[1792,8,72]{0,2,1:T(8,128)(2,1)} reshape(bf16[8,224,576]{1,0,2:T(8,128)(2,1)} %copy.35) | data formatting | bytes 4128768 | tf_op jit(solution)/shard_map/reshape;reshape | solution.py:56
  107.9 3.2 %copy.34 = bf16[1792,576]{0,1:T(8,128)(2,1)S(1)} copy(bf16[1792,576]{1,0:T(8,128)(2,1)} %all-gather.2.cloned.1.call-done) | data formatting | bytes 4128768 | tf_op jit(solution)/shard_map/all_gather | solution.py:49
  111.1 2.9 %multiply_reduce_fusion = (f32[8,224]{1,0:T(8,128)S(1)}, f32[8,224,1792]{2,1,0:T(8,128)S(1)}) fusion(bf16[224,8,72]{0,2,1:T(8,128)(2,1)} %bitcast.87, bf16[1792,8,72]{0,2,1:T(8,128)(2,1)S(1)} %bitcast.84), kind=kOutput, calls=%fused_computation.1 | convolution fusion | flops 468842752 | bytes 15174656 | tf_op jit(solution)/shard_map/qhd,khd->hqk/dot_general | solution.py:58
  114.1 2.3 %fusion = f32[8,224]{1,0:T(8,128)S(1)} fusion(f32[8,224,1792]{2,1,0:T(8,128)S(1)} %get-tuple-element.20, f32[8,224]{1,0:T(8,128)S(1)} %broadcast_maximum_fusion), kind=kLoop, calls=%fused_computation.2 | loop fusion | flops 9632000 | bytes 12859392 | tf_op jit(solution)/shard_map/reduce_sum | solution.py:63
  116.3 2.3 %copy-done.1 = f32[8,224,1792]{2,1,0:T(8,128)} copy-done((f32[8,224,1792]{2,1,0:T(8,128)}, f32[8,224,1792]{2,1,0:T(8,128)S(1)}, u32[]{:S(2)}) %copy-start.1) | copy-done | bytes 12845080
  118.7 7.8 %fusion.45 = bf16[224,8,72]{0,2,1:T(8,128)(2,1)S(1)} fusion(bf16[1792,8,72]{0,2,1:T(8,128)(2,1)} %reshape_reshape.3, f32[8,224,1792]{2,1,0:T(8,128)} %copy-done.1, f32[8,224]{1,0:T(8,128)S(1)} %broadcast_maximum_fusion, f32[224,8]{0,1:T(8,128)S(1)} %bitcast.89), kind=kOutput, calls=%fused_computation.54 | convolution fusion | flops 472313856 | bytes 15181824 | tf_op jit(solution)/shard_map/hqk,khd->hqd/dot_general | solution.py:64
  126.5 2.0 fusion.10
  128.4 2.8 %copy.59 = bf16[1,448,1152]{2,0,1:T(2,128)(2,1)S(1)} copy(bf16[1,448,1152]{2,1,0:T(8,128)(2,1)} %fusion.10) | data formatting | bytes 2064384 | tf_op jit(solution)/shard_map/broadcast_in_dim | solution.py:82
  131.8 8.2 %reduce.17 = bf16[448,1152]{1,0:T(8,128)(2,1)} reduce(bf16[448,1,1152]{2,1,0:T(2,128)(2,1)S(1)} %bitcast.85, bf16[]{:T(256)} %broadcast.88), dimensions={1}, to_apply=%bitcast.83.reduce_sub_computation | reduce | bytes 2064386
  140.0 2.4 %reshape.106 = bf16[32,2,8064]{2,1,0:T(2,128)(2,1)S(1)} reshape(bf16[448,1152]{1,0:T(8,128)(2,1)} %reduce.17) | data formatting | bytes 2064384
  142.4 22.0 %all_to_all.26 = bf16[32,2,8064]{2,1,0:T(2,128)(2,1)} all-to-all(bf16[32,2,8064]{2,1,0:T(2,128)(2,1)S(1)} %reshape.106), channel_id=1, replica_groups=mesh['frames'=32,'space'=8] {'frames'}, dimensions={0} | all-to-all | bytes 2064384 | tf_op jit(solution)/shard_map/all_to_all | solution.py:81
  164.4 4.2 %reshape.107 = bf16[448,1,1152]{2,1,0:T(2,128)(2,1)S(1)} reshape(bf16[32,2,8064]{2,1,0:T(2,128)(2,1)} %all_to_all.26) | data formatting | bytes 2064384
  169.8 1.3 copy-done.10
  171.1 2.5 %convolution_convert_fusion = bf16[448,1728]{1,0:T(8,128)(2,1)S(1)} fusion(bf16[1152,1728]{0,1:T(8,128)(2,1)S(1)} %copy-done.10, bf16[1,448,1152]{2,1,0:T(8,128)(2,1)S(1)} %get-tuple-element.12, f32[1152]{0:T(1024)S(1)} %copy-done.6, f32[1152]{0:T(1024)S(1)} %copy-done.7, f32[448]{0:T(512)S(1)} %add_rsqrt_fusion, f32[448]{0:T(512)S(1)} %broadcast_multiply_fusion), kind=kOutput, calls=%fused_computation.14 | convolution fusion | flops 1787498496 | bytes 6574592 | tf_op jit(solution)/shard_map/dot_general | solution.py:88
  173.6 4.0 %reshape.96 = bf16[32,14,3,8,72]{4,3,2,1,0:T(8,128)(2,1)} reshape(bf16[448,1728]{1,0:T(8,128)(2,1)S(1)} %convolution_convert_fusion) | data formatting | bytes 3096576 | tf_op jit(solution)/shard_map/reshape | solution.py:91
  177.6 1.9 fusion.61
  180.7 1.1 fusion.26
  182.2 1.5 reshape.97
  183.7 2.5 %fusion.8 = bf16[448,1152]{1,0:T(8,128)(2,1)S(1)} fusion(bf16[448,576]{1,0:T(8,128)(2,1)} %reshape.97, bf16[576,1152]{1,0:T(8,128)(2,1)} %param.13, bf16[1,448,1152]{2,1,0:T(8,128)(2,1)S(1)} %copy-done.5, f32[1152]{0:T(1024)S(1)} %get-tuple-element.5), kind=kOutput, calls=%fused_computation.15 | convolution fusion | flops 596606976 | bytes 3912192 | tf_op jit(solution)/shard_map/dot_general | solution.py:110
  186.6 18.5 %all_to_all.27 = bf16[32,14,1152]{2,1,0:T(8,128)(2,1)} all-to-all(bf16[32,14,1152]{2,1,0:T(8,128)(2,1)S(1)} %reshape.98), channel_id=1, replica_groups=mesh['frames'=32,'space'=8] {'frames'}, dimensions={0} | all-to-all | bytes 2064384 | tf_op jit(solution)/shard_map/all_to_all | solution.py:116
  205.1 2.2 %all_to_all.22 = bf16[1,448,1152]{2,1,0:T(8,128)(2,1)} reshape(bf16[32,14,1152]{2,1,0:T(8,128)(2,1)} %all_to_all.27) | data formatting | bytes 2064384 | tf_op jit(solution)/shard_map/all_to_all | solution.py:116
  (36 shorter events, 3.9 us)
Async XLA Ops:
  6.5 119.9 %copy-start = (bf16[576,1152]{1,0:T(8,128)(2,1)S(1)}, bf16[576,1152]{1,0:T(8,128)(2,1)}, u32[]{:S(2)}) copy-start(bf16[576,1152]{1,0:T(8,128)(2,1)} %param.11) | copy-start | bytes 3981316
  6.5 5.0 %copy-start.2 = (bf16[1,448,1152]{2,1,0:T(8,128)(2,1)S(1)}, bf16[1,448,1152]{2,1,0:T(8,128)(2,1)}, u32[]{:S(2)}) copy-start(bf16[1,448,1152]{2,1,0:T(8,128)(2,1)} %param.7) | copy-start | bytes 3096580
  6.5 4.8 %copy-start.9 = (s32[1,448]{1,0:T(1,128)S(1)}, s32[1,448]{1,0:T(1,128)}, u32[]{:S(2)}) copy-start(s32[1,448]{1,0:T(1,128)} %param.8) | copy-start | bytes 5380
  18.1 79.7 %all-to-all-start = ((bf16[8,224,576]{2,1,0:T(8,128)(2,1)}), bf16[8,224,576]{2,1,0:T(8,128)(2,1)}, u32[]{:S(2)}, u32[]{:S(2)}) async-start(bf16[8,224,576]{2,1,0:T(8,128)(2,1)} %stack.2), calls=%async_computation | async-start | bytes 4587520 | tf_op jit(solution)/shard_map/all_to_all | solution.py:51
  26.5 81.4 %all-gather.2.cloned.1.call-start = ((), (), s32[]{:S(2)}) async-start(), calls=%async_computation.3 | async-start | bytes 2580480 | tf_op jit(solution)/shard_map/all_gather | solution.py:49
  114.0 4.6 %copy-start.1 = (f32[8,224,1792]{2,1,0:T(8,128)}, f32[8,224,1792]{2,1,0:T(8,128)S(1)}, u32[]{:S(2)}) copy-start(f32[8,224,1792]{2,1,0:T(8,128)S(1)} %get-tuple-element.20) | copy-start | bytes 38535172
  118.6 7.8 %copy-start.3 = (bf16[1,448,1152]{2,1,0:T(8,128)(2,1)S(1)}, bf16[1,448,1152]{2,1,0:T(8,128)(2,1)}, u32[]{:S(2)}) copy-start(bf16[1,448,1152]{2,1,0:T(8,128)(2,1)} %param.7) | copy-start | bytes 3096580
  118.7 7.8 %copy-start.8 = (f32[1152]{0:T(1024)S(1)}, f32[1152]{0:T(1024)}, u32[]{:S(2)}) copy-start(f32[1152]{0:T(1024)} %get-tuple-element.8) | copy-start | bytes 13828
  168.6 1.2 copy-start.6
  168.6 1.2 copy-start.7
  168.6 2.5 %copy-start.10 = (bf16[1152,1728]{0,1:T(8,128)(2,1)S(1)}, bf16[1152,1728]{0,1:T(8,128)(2,1)}, u32[]{:S(2)}) copy-start(bf16[1152,1728]{0,1:T(8,128)(2,1)} %param.12) | copy-start | bytes 11943940
  168.9 1.0 copy-start.4
  181.8 1.9 copy-start.5
Sparse Core Ops, SparseCore 0:
  29.2 69.5 all-gather.1
